TPU v7x, 128 devices: a whole 4x4x4 slice. The times are simulated.
128 devices in a mesh: gx: 8 (over y, x_hi), gy: 4 (over x_lo, core), gz: 4 (over z).
Axes of the slice: x: 4 (x_hi: 2, x_lo: 2; x = x_hi * 2 + x_lo), y: 4, z: 4, core: 2. Of those that a mesh axis runs over, the one named last changes fastest.
Arguments:
- field: float32 [1024, 256, 512], P('gx', 'gy', 'gz'), may hold values from -1 to 1, as said below
- start_basis: float32 [1024, 128], replicated, may hold values from -6 to 6
Outputs:
- scaled_basis: float32 [1024, 128], P('gx')
- core: float32 [128, 256, 512], P('gx', 'gy', 'gz')
Inputs may be any that keep to these rules, and one draw needn't show every extreme that they name: `field`: real values of varying scale over rows and columns.
All inputs are finite; a program needn't handle non-finite values.
Results may differ from a plain program's by a relative error of at most 0.00027.
Values sent between devices are 32-bit elements; how exact they have to be, the bound alone decides.
A program may use at most 64 MiB of HBM per device.

v0:
```python
import jax
import jax.numpy as jnp
from jax import lax
from jax.sharding import PartitionSpec as P

ITERS = 8


def orthonormal(image, products):
    lower = jnp.linalg.cholesky(products)
    return lax.linalg.triangular_solve(lower, image, left_side=False, lower=True, transpose_a=True)


def body(field, start_basis):
    hi = lax.Precision.HIGHEST
    rows_x, cells_y, cells_z = field.shape
    flat = field.reshape(rows_x, cells_y * cells_z)
    fibres = lax.all_to_all(flat, "gx", split_axis=1, concat_axis=0, tiled=True)
    partial_gram = jnp.dot(fibres, fibres.T, precision=hi, preferred_element_type=jnp.float32)
    basis = start_basis
    gram = lax.psum(partial_gram, ("gx", "gy", "gz"))
    for step in range(ITERS):
        image = jnp.dot(gram, basis, precision=hi, preferred_element_type=jnp.float32)
        products = jnp.dot(image.T, image, precision=hi, preferred_element_type=jnp.float32)
        basis = orthonormal(image, products)
    own_rows = lax.dynamic_slice_in_dim(basis, lax.axis_index("gx") * rows_x, rows_x, 0)
    scaled_basis = own_rows * jnp.sqrt(jnp.float32(basis.shape[0]))
    flipped = own_rows.T
    core_rows = lax.psum_scatter(
        jnp.dot(flipped, flat, precision=hi, preferred_element_type=jnp.float32),
        "gx",
        scatter_dimension=0,
        tiled=True,
    )
    core = core_rows.reshape(core_rows.shape[0], cells_y, cells_z)
    return (scaled_basis, core)


def solution(mesh):
    placed = (P("gx", "gy", "gz"), P())
    return jax.shard_map(
        body,
        mesh=mesh,
        in_specs=placed,
        out_specs=(P("gx", None), P("gx", "gy", "gz")),
        check_vma=False,
    )
```

profile of v0, /device:TPU:1, one launch (start us, length us, event | category | flops | bytes accessed | tf_op | source)
XLA Modules:
  0.0 589.8 jit_solution(754648791435392846)
XLA Ops:
  7.2 5.5 copy.22
  12.7 57.6 %all_to_all.19 = f32[128,8,1024]{0,2,1:T(8,128)} all-to-all(f32[128,8,1024]{0,2,1:T(8,128)} %bitcast.141), channel_id=1, replica_groups=mesh['gx'=8,'gy'=4,'gz'=4] {'gx'}, dimensions={1} | all-to-all | bytes 8388608 | tf_op jit(solution)/shard_map/all_to_all | solution.py:18
  70.3 5.3 copy.23
  75.7 18.1 %fusion.43 = f32[1024,1024]{1,0:T(8,128)} fusion(f32[1024,1024]{1,0:T(8,128)} %bitcast.142), kind=kOutput, calls=%fused_computation.79 | convolution fusion | flops 12884901888 | bytes 8388608 | tf_op jit(solution)/shard_map/dot_general | solution.py:19
  94.1 153.8 %all-reduce.2.cloned.1.call-done = f32[1024,1024]{1,0:T(8,128)} async-done(((f32[1024,1024]{1,0:T(8,128)}), f32[1024,1024]{1,0:T(8,128)}) %all-reduce.2.cloned.1.call-update) | async-done | bytes 4194320 | tf_op jit(solution)/shard_map/psum | solution.py:21
  247.9 5.2 fusion.44
  254.2 11.7 %cholesky.134 = f32[128,128]{1,0:T(8,128)S(1)} custom-call(f32[128,128]{1,0:T(8,128)S(1)} %fusion.26), custom_call_target="Cholesky" | custom-call | tf_op jit(solution)/shard_map/jit(cholesky)/cholesky | solution.py:10
  267.3 9.8 %custom-call.12 = f32[1,128,128]{1,2,0:T(8,128)S(1)} custom-call(f32[1,128,128]{2,1,0:T(8,128)S(1)} %fusion.3), custom_call_target="InvertDiagBlocksLowerTriangular" | custom-call | tf_op jit(solution)/shard_map/triangular_solve/custom-call.0 | solution.py:11
  277.7 5.6 fusion.46
  284.5 11.7 %cholesky.145 = f32[128,128]{1,0:T(8,128)S(1)} custom-call(f32[128,128]{1,0:T(8,128)S(1)} %fusion.24), custom_call_target="Cholesky" | custom-call | tf_op jit(solution)/shard_map/jit(cholesky)/cholesky | solution.py:10
  297.6 9.8 %custom-call.13 = f32[1,128,128]{1,2,0:T(8,128)S(1)} custom-call(f32[1,128,128]{2,1,0:T(8,128)S(1)} %fusion.4), custom_call_target="InvertDiagBlocksLowerTriangular" | custom-call | tf_op jit(solution)/shard_map/triangular_solve/custom-call.0 | solution.py:11
  308.0 5.4 fusion.48
  314.6 11.7 %cholesky.156 = f32[128,128]{1,0:T(8,128)S(1)} custom-call(f32[128,128]{1,0:T(8,128)S(1)} %fusion.22), custom_call_target="Cholesky" | custom-call | tf_op jit(solution)/shard_map/jit(cholesky)/cholesky | solution.py:10
  327.6 9.8 %custom-call.14 = f32[1,128,128]{1,2,0:T(8,128)S(1)} custom-call(f32[1,128,128]{2,1,0:T(8,128)S(1)} %fusion.5), custom_call_target="InvertDiagBlocksLowerTriangular" | custom-call | tf_op jit(solution)/shard_map/triangular_solve/custom-call.0 | solution.py:11
  338.1 5.4 fusion.50
  344.6 11.7 %cholesky.167 = f32[128,128]{1,0:T(8,128)S(1)} custom-call(f32[128,128]{1,0:T(8,128)S(1)} %fusion.20), custom_call_target="Cholesky" | custom-call | tf_op jit(solution)/shard_map/jit(cholesky)/cholesky | solution.py:10
  357.7 9.8 %custom-call.15 = f32[1,128,128]{1,2,0:T(8,128)S(1)} custom-call(f32[1,128,128]{2,1,0:T(8,128)S(1)} %fusion.6), custom_call_target="InvertDiagBlocksLowerTriangular" | custom-call | tf_op jit(solution)/shard_map/triangular_solve/custom-call.0 | solution.py:11
  368.2 5.6 fusion.52
  374.9 11.7 %cholesky.178 = f32[128,128]{1,0:T(8,128)S(1)} custom-call(f32[128,128]{1,0:T(8,128)S(1)} %fusion.18), custom_call_target="Cholesky" | custom-call | tf_op jit(solution)/shard_map/jit(cholesky)/cholesky | solution.py:10
  388.0 9.8 %custom-call.16 = f32[1,128,128]{1,2,0:T(8,128)S(1)} custom-call(f32[1,128,128]{2,1,0:T(8,128)S(1)} %fusion.7), custom_call_target="InvertDiagBlocksLowerTriangular" | custom-call | tf_op jit(solution)/shard_map/triangular_solve/custom-call.0 | solution.py:11
  398.4 5.4 fusion.54
  405.0 11.7 %cholesky.189 = f32[128,128]{1,0:T(8,128)S(1)} custom-call(f32[128,128]{1,0:T(8,128)S(1)} %fusion.16), custom_call_target="Cholesky" | custom-call | tf_op jit(solution)/shard_map/jit(cholesky)/cholesky | solution.py:10
  418.0 9.8 %custom-call.17 = f32[1,128,128]{1,2,0:T(8,128)S(1)} custom-call(f32[1,128,128]{2,1,0:T(8,128)S(1)} %fusion.8), custom_call_target="InvertDiagBlocksLowerTriangular" | custom-call | tf_op jit(solution)/shard_map/triangular_solve/custom-call.0 | solution.py:11
  428.5 5.4 fusion.56
  435.1 11.7 %cholesky.200 = f32[128,128]{1,0:T(8,128)S(1)} custom-call(f32[128,128]{1,0:T(8,128)S(1)} %fusion.14), custom_call_target="Cholesky" | custom-call | tf_op jit(solution)/shard_map/jit(cholesky)/cholesky | solution.py:10
  448.1 9.8 %custom-call.18 = f32[1,128,128]{1,2,0:T(8,128)S(1)} custom-call(f32[1,128,128]{2,1,0:T(8,128)S(1)} %fusion.9), custom_call_target="InvertDiagBlocksLowerTriangular" | custom-call | tf_op jit(solution)/shard_map/triangular_solve/custom-call.0 | solution.py:11
  458.6 5.5 fusion.58
  465.2 11.7 %cholesky.211 = f32[128,128]{1,0:T(8,128)S(1)} custom-call(f32[128,128]{1,0:T(8,128)S(1)} %fusion.12), custom_call_target="Cholesky" | custom-call | tf_op jit(solution)/shard_map/jit(cholesky)/cholesky | solution.py:10
  478.2 9.8 %custom-call.19 = f32[1,128,128]{1,2,0:T(8,128)S(1)} custom-call(f32[1,128,128]{2,1,0:T(8,128)S(1)} %fusion.10), custom_call_target="InvertDiagBlocksLowerTriangular" | custom-call | tf_op jit(solution)/shard_map/triangular_solve/custom-call.0 | solution.py:11
  488.7 9.9 %fusion = f32[128,8192]{1,0:T(8,128)} fusion(f32[16,8,64,128]{3,2,1,0:T(8,128)} %bitcast.139, f32[1024,128]{0,1:T(8,128)S(1)} %convolution_bitcast_fusion, s32[]{:T(128)S(6)} %select_n.6), kind=kOutput, calls=%fused_computation | convolution fusion | flops 1610612736 | bytes 8454148 | tf_op jit(solution)/shard_map/dot_general | solution.py:30
  499.4 81.2 %reduce-scatter.2.cloned.1.call-done = f32[16,8192]{1,0:T(8,128)} async-done(((f32[128,8192]{1,0:T(8,128)}), f32[16,8192]{1,0:T(8,128)}) %reduce-scatter.2.cloned.1.call-update) | async-done | bytes 524304 | tf_op jit(solution)/shard_map/reduce_scatter | solution.py:29
  580.6 1.9 copy.34
  (64 shorter events, 25.8 us)
Async XLA Ops:
  7.2 240.7 %copy-start = (f32[1024,128]{1,0:T(8,128)S(1)}, f32[1024,128]{1,0:T(8,128)}, u32[]{:S(2)}) copy-start(f32[1024,128]{1,0:T(8,128)} %param.6) | copy-start | bytes 1572868
  7.2 240.7 %all-reduce.2.cloned.1.call-start = ((), (), s32[]{:S(2)}) async-start(), calls=%async_computation.2 | async-start | bytes 8388608 | tf_op jit(solution)/shard_map/psum | solution.py:21
  93.8 486.8 %reduce-scatter.2.cloned.1.call-start = ((), (), s32[]{:S(2)}) async-start(), calls=%async_computation.3 | async-start | bytes 4718592 | tf_op jit(solution)/shard_map/reduce_scatter | solution.py:29
Sparse Core Ops, SparseCore 0:
  93.9 153.8 all-reduce.1
  498.7 81.8 reduce-scatter.1
where the time goes:
time: 597 us; the launch traced here: 590 us
  waiting for transfers between devices  235 us (39%)
  other arithmetic  183 us (31%)
  matrix products  84.8 us (14%)
  blocking collectives  57.6 us (10%)
  between operations  14.9 us (2%)
  local copies, waits for them, and re-layouts  14.2 us (2%)
    psum x1, waiting for transfers between devices, body(): gram = lax.psum(partial_gram, ('gx', 'gy', 'gz'))  154 us
    another operation x24, other arithmetic, orthonormal(): lower = jnp.linalg.cholesky(products)  99.1 us
    another operation x16, other arithmetic, orthonormal(): lax.linalg.triangular_solve(lower, image, left_side=False, lower=True, tr...  83.7 us
    reduce_scatter x1, waiting for transfers between devices, body(): lax.psum_scatter(jnp.dot(flipped, flat, precision=hi, preferred_element_t...  81.2 us
    all_to_all x1, blocking collectives, body(): fibres = lax.all_to_all(flat, 'gx', split_axis=1, concat_axis=0, tiled=True)  57.6 us
    dot_general x8, matrix products, body(): jnp.dot(gram, basis, precision=hi, preferred_element_type=jnp.float32)  43.6 us
    dot_general x1, matrix products, body(): jnp.dot(fibres, fibres.T, precision=hi, preferred_element_type=jnp.float32)  18.1 us
  transfers between devices with their start and end apart: 2, of which 2 were waited for; matrix products, arithmetic and copies ran while one was open for 0% of the time, Pallas kernels for 0%

commit v1 on v0

v1 whole, which is shorter than its diff:
```python
import functools

import jax
import jax.numpy as jnp
from jax import lax
from jax.experimental import pallas as pl
from jax.experimental.pallas import tpu as pltpu
from jax.sharding import PartitionSpec as P

ITERS = 8
F32 = jnp.float32
BF16 = jnp.bfloat16


def split(x):
    high = x.astype(BF16)
    return high, (x - high.astype(F32)).astype(BF16)


def dg(a, b, ca, cb):
    return lax.dot_general(a, b, (((ca,), (cb,)), ((), ())), preferred_element_type=F32)


def lower_inverse(aug, panel=8):
    n = aug.shape[0]
    row = lax.broadcasted_iota(jnp.int32, (panel, n), 0)
    for first in range(0, n, panel):
        left, right = aug[first : first + panel, :n], aug[first : first + panel, n:]
        cols = [jnp.broadcast_to(left[:, first + k : first + k + 1], (panel, n)) for k in range(panel)]
        pivots = None
        for i in range(panel):
            pivot = jnp.broadcast_to(cols[i][i : i + 1, :], (panel, n))
            ratio = jnp.where(row > i, cols[i], 0.0) * (1.0 / pivot)
            for k in range(i + 1, panel):
                cols[k] = cols[k] - ratio * jnp.broadcast_to(cols[k][i : i + 1, :], (panel, n))
            left = left - ratio * jnp.broadcast_to(left[i : i + 1, :], (panel, n))
            right = right - ratio * jnp.broadcast_to(right[i : i + 1, :], (panel, n))
            pivots = pivot if pivots is None else jnp.where(row == i, pivot, pivots)
        scale = lax.rsqrt(pivots)
        left, right = left * scale, right * scale
        aug[first : first + panel, n:] = right
        if first + panel < n:
            update = lax.dot_general(
                left,
                jnp.concatenate([left, right], axis=1),
                (((0,), (0,)), ((), ())),
                precision=lax.Precision.HIGHEST,
                preferred_element_type=F32,
            )
            aug[first + panel :, :] = aug[first + panel :, :] - update[first + panel :, :]


def iteration_kernel(gram_ref, start_ref, out_ref, gram_high, gram_low, aug, basis):
    high, low = split(gram_ref[...])
    gram_high[...] = high
    gram_low[...] = low
    basis[...] = start_ref[...]
    n = aug.shape[0]
    shape = (n, n)
    eye = (lax.broadcasted_iota(jnp.int32, shape, 0) == lax.broadcasted_iota(jnp.int32, shape, 1)).astype(F32)

    def step(_, carry):
        bh, bl = split(basis[...])
        both = dg(gram_high[...], jnp.concatenate([bh, bl], axis=1), 1, 0)
        image = both[:, :n] + both[:, n:] + dg(gram_low[...], bh, 1, 0)
        ih, il = split(image)
        both = dg(ih, jnp.concatenate([ih, il], axis=1), 0, 0)
        mixed = both[:, n:]
        aug[:, :n] = both[:, :n] + mixed + mixed.T
        aug[:, n:] = eye
        lower_inverse(aug)
        th, tl = split(aug[:, n:])
        both = dg(ih, jnp.concatenate([th, tl], axis=0), 1, 1)
        basis[...] = both[:, :n] + both[:, n:] + dg(il, th, 1, 1)
        return carry

    lax.fori_loop(0, ITERS, step, 0)
    out_ref[...] = basis[...]


def iterate(gram, start):
    order, rank = start.shape
    return pl.pallas_call(
        iteration_kernel,
        out_shape=jax.ShapeDtypeStruct((order, rank), F32),
        in_specs=[pl.BlockSpec(memory_space=pltpu.VMEM)] * 2,
        out_specs=pl.BlockSpec(memory_space=pltpu.VMEM),
        scratch_shapes=[
            pltpu.VMEM((order, order), BF16),
            pltpu.VMEM((order, order), BF16),
            pltpu.VMEM((rank, 2 * rank), F32),
            pltpu.VMEM((order, rank), F32),
        ],
        compiler_params=pltpu.CompilerParams(vmem_limit_bytes=48 << 20),
    )(gram, start)


def body(field, start_basis):
    rows_x, cells_y, cells_z = field.shape
    flat = field.reshape(rows_x, cells_y * cells_z)
    fibres = lax.all_to_all(flat, "gx", split_axis=1, concat_axis=0, tiled=True)
    partial_gram = jnp.dot(fibres, fibres.T, precision=lax.Precision.HIGH, preferred_element_type=F32)
    gram = lax.psum(partial_gram, ("gx", "gy", "gz"))
    basis = iterate(gram, start_basis)
    own_rows = lax.dynamic_slice_in_dim(basis, lax.axis_index("gx") * rows_x, rows_x, 0)
    scaled_basis = own_rows * jnp.sqrt(jnp.float32(basis.shape[0]))
    core_cols = jnp.dot(basis.T, fibres, precision=lax.Precision.HIGH, preferred_element_type=F32)
    core = lax.all_to_all(core_cols, "gx", split_axis=0, concat_axis=1, tiled=True)
    return (scaled_basis, core.reshape(core.shape[0], cells_y, cells_z))


def solution(mesh):
    placed = (P("gx", "gy", "gz"), P())
    return jax.shard_map(
        body,
        mesh=mesh,
        in_specs=placed,
        out_specs=(P("gx", None), P("gx", "gy", "gz")),
        check_vma=False,
    )
```

time: 597 us -> 354 us (0.59)
  other arithmetic: 183 us -> 0.63 us
  Pallas kernels: 0 us -> 84.5 us
  matrix products: 84.8 us -> 12.6 us
  waiting for transfers between devices: 235 us -> 163 us
    another operation x40 -> x0, other arithmetic: 183 us -> none  [the longest x24 99.1 us: orthonormal(): lower = jnp.linalg.cholesky(products)]
    pallas_call x0 -> x1, Pallas kernels: none -> 84.5 us  [iterate(): pl.pallas_call(iteration_kernel, out_shape=jax.ShapeDtypeStruct((order, r...]
    reduce_scatter x1 -> x0, waiting for transfers between devices: 81.2 us -> none  [body(): lax.psum_scatter(jnp.dot(flipped, flat, precision=hi, preferred_element_t...]
    dot_general x18 -> x2, matrix products: 79.7 us -> 12.6 us  [the longest x1 8.31 us: body(): jnp.dot(fibres, fibres.T, precision=lax.Precision.HIGH, preferred_element...]
    all_to_all x0 -> x1, waiting for transfers between devices: none -> 9.23 us  [body(): lax.all_to_all(core_cols, 'gx', split_axis=0, concat_axis=1, tiled=True)]
where the time goes in v1:
time: 354 us; the launch traced here: 352 us
  waiting for transfers between devices  163 us (46%)
  Pallas kernels  84.5 us (24%)
  blocking collectives  57.3 us (16%)
  local copies, waits for them, and re-layouts  15 us (4%)
  between operations  14.1 us (4%)
  matrix products  12.6 us (4%)
  starting transfers between devices  4.76 us (1%)
    psum x1, waiting for transfers between devices, body(): gram = lax.psum(partial_gram, ('gx', 'gy', 'gz'))  154 us
    pallas_call x1, Pallas kernels, iterate(): pl.pallas_call(iteration_kernel, out_shape=jax.ShapeDtypeStruct((order, r...  84.5 us
    all_to_all x1, blocking collectives, body(): fibres = lax.all_to_all(flat, 'gx', split_axis=1, concat_axis=0, tiled=True)  57.3 us
    all_to_all x2, local copies, waits for them, and re-layouts, body(): fibres = lax.all_to_all(flat, 'gx', split_axis=1, concat_axis=0, tiled=True)  9.49 us
    all_to_all x1, waiting for transfers between devices, body(): lax.all_to_all(core_cols, 'gx', split_axis=0, concat_axis=1, tiled=True)  9.23 us
    dot_general x1, matrix products, body(): jnp.dot(fibres, fibres.T, precision=lax.Precision.HIGH, preferred_element...  8.31 us
  transfers between devices with their start and end apart: 2, of which 2 were waited for; matrix products, arithmetic and copies ran while one was open for 0% of the time, Pallas kernels for 0%

profile of v1, /device:TPU:1, one launch (start us, length us, event | category | flops | bytes accessed | tf_op | source)
XLA Modules:
  0.0 352.2 jit_solution(14161597503560938287)
XLA Ops:
  7.2 0.0 all-reduce.2.cloned.1.call-start
  7.2 4.9 %all_to_all.24 = f32[128,8,1024]{2,1,0:T(8,128)} reshape(f32[128,64,128]{2,1,0:T(8,128)} %param.2) | data formatting | bytes 8388608 | tf_op jit(solution)/shard_map/all_to_all | solution.py:101
  12.1 4.6 %copy.6 = f32[128,8,1024]{2,0,1:T(8,128)S(1)} copy(f32[128,8,1024]{2,1,0:T(8,128)} %all_to_all.24) | data formatting | bytes 8388608 | tf_op jit(solution)/shard_map/all_to_all | solution.py:101
  16.7 57.3 %all_to_all.32 = f32[128,8,1024]{2,0,1:T(8,128)S(1)} all-to-all(f32[128,8,1024]{2,0,1:T(8,128)S(1)} %copy.6), channel_id=1, replica_groups=mesh['gx'=8,'gy'=4,'gz'=4] {'gx'}, dimensions={1} | all-to-all | bytes 8388608 | tf_op jit(solution)/shard_map/all_to_all | solution.py:101
  74.0 0.0 copy-start.2
  74.0 1.9 copy-done.2
  76.0 8.3 %fusion = f32[1024,1024]{1,0:T(8,128)} fusion(f32[1024,1024]{1,0:T(8,128)S(1)} %bitcast.13), kind=kOutput, calls=%fused_computation.1 | convolution fusion | flops 6442450944 | bytes 8388608 | tf_op jit(solution)/shard_map/dot_general | solution.py:102
  84.3 0.0 copy-start.1
  84.3 0.0 all-reduce.2.cloned.1.call-update
  84.3 154.0 %all-reduce.2.cloned.1.call-done.gram_ref = f32[1024,1024]{1,0:T(8,128)} async-done(((f32[1024,1024]{1,0:T(8,128)}), f32[1024,1024]{1,0:T(8,128)}) %all-reduce.2.cloned.1.call-update) | async-done | bytes 4194320 | tf_op jit(solution)/shard_map/psum | solution.py:103
  238.3 0.0 copy-done.1
  238.3 0.0 copy-start
  238.3 2.2 copy-done
  240.5 84.5 %shard_map.41 = f32[1024,128]{1,0:T(8,128)S(1)} custom-call(f32[1024,1024]{1,0:T(8,128)S(1)} %copy-done, f32[1024,128]{1,0:T(8,128)S(1)} %copy-done.1), custom_call_target="tpu_custom_call" | custom-call | tf_op jit(solution)/shard_map/pallas_call | solution.py:83
  325.1 0.2 copy.7
  325.3 4.3 %fusion.1 = f32[8,16,1024]{2,1,0:T(8,128)} fusion(f32[8,16,1024]{2,1,0:T(8,128)S(1)} %bitcast.15, f32[1024,1024,1]{1,0,2:T(8,128)} %bitcast.14), kind=kOutput, calls=%fused_computation.2 | convolution fusion | flops 805306368 | bytes 5242880 | tf_op jit(solution)/shard_map/dot_general | solution.py:107
  329.6 4.7 %all-to-all-start.1 = ((f32[8,16,1024]{2,1,0:T(8,128)}), f32[8,16,1024]{2,1,0:T(8,128)S(1)}, u32[]{:S(2)}, u32[]{:S(2)}) async-start(f32[8,16,1024]{2,1,0:T(8,128)} %fusion.1), calls=%async_computation.1 | async-start | bytes 1048576 | tf_op jit(solution)/shard_map/all_to_all | solution.py:108
  334.3 0.6 dynamic-slice_multiply_fusion
  334.9 9.2 %all-to-all-done.1 = f32[8,16,1024]{2,1,0:T(8,128)S(1)} async-done(((f32[8,16,1024]{2,1,0:T(8,128)}), f32[8,16,1024]{2,1,0:T(8,128)S(1)}, u32[]{:S(2)}, u32[]{:S(2)}) %all-to-all-start.1) | async-done | bytes 524320 | tf_op jit(solution)/shard_map/all_to_all | solution.py:108
  344.2 0.3 copy.8
  344.5 0.9 reshape.17
Async XLA Ops:
  7.2 231.2 %all-reduce.2.cloned.1.call-start = ((), (), s32[]{:S(2)}) async-start(), calls=%async_computation.2 | async-start | bytes 8388608 | tf_op jit(solution)/shard_map/psum | solution.py:103
  74.0 1.9 copy-start.2
  84.3 154.1 %copy-start.1 = (f32[1024,128]{1,0:T(8,128)S(1)}, f32[1024,128]{1,0:T(8,128)}, u32[]{:S(2)}) copy-start(f32[1024,128]{1,0:T(8,128)} %start_ref.1) | copy-start | bytes 1572868
  238.3 2.2 copy-start
  329.6 14.6 %all-to-all-start.1 = ((f32[8,16,1024]{2,1,0:T(8,128)}), f32[8,16,1024]{2,1,0:T(8,128)S(1)}, u32[]{:S(2)}, u32[]{:S(2)}) async-start(f32[8,16,1024]{2,1,0:T(8,128)} %fusion.1), calls=%async_computation.1 | async-start | bytes 1048576 | tf_op jit(solution)/shard_map/all_to_all | solution.py:108
Sparse Core Ops, SparseCore 0:
  84.4 153.8 all-reduce.1

commit v2 on v1

--- a/solution.py
+++ b/solution.py
@@ -8,6 +8,7 @@
 from jax.sharding import PartitionSpec as P
 
 ITERS = 8
+MESH = pl.DeviceIdType.MESH
 F32 = jnp.float32
 BF16 = jnp.bfloat16
 
@@ -50,10 +51,234 @@
             aug[first + panel :, :] = aug[first + panel :, :] - update[first + panel :, :]
 
 
+class Place:
+    def __init__(self):
+        gx, gy = lax.axis_index("gx"), lax.axis_index("gy")
+        self.gx, self.gy = gx, gy
+        self.core = gy % 2
+        self.at = {"x": (gx % 2) * 2 + gy // 2, "y": gx // 2, "z": lax.axis_index("gz")}
+
+    def along(self, axis, step):
+        to = (self.at[axis] + step) % 4
+        if axis == "z":
+            return {"gz": to}
+        if axis == "y":
+            return {"gx": to * 2 + self.gx % 2}
+        return {"gx": self.at["y"] * 2 + to // 2, "gy": (to % 2) * 2 + self.core}
+
+    def partner(self):
+        return {"gy": self.gy - self.core + 1 - self.core}
+
+
+def greet(peers):
+    barrier = pltpu.get_barrier_semaphore()
+    for peer in peers:
+        pl.semaphore_signal(barrier, inc=1, device_id=peer, device_id_type=MESH)
+    pl.semaphore_wait(barrier, len(peers))
+
+
+def push(src, dst, sems, k, peer):
+    copy = pltpu.make_async_remote_copy(
+        src_ref=src, dst_ref=dst, send_sem=sems.at[0, k], recv_sem=sems.at[1, k], device_id=peer, device_id_type=MESH
+    )
+    copy.start()
+    return copy
+
+
+STREAMS = (("z", "y", "x"), ("y", "x", "z"), ("x", "z", "y"))
+HALF, THIRD, PIECE, BIT = 2304, 768, 192, 48
+A2A_ORDER = (1, 2, 6, 4, 5, 3, 7)
+
+
+def first_row(i, j):
+    return (i * (i + 1) // 2 + j) * 128
+
+
+def gather_products(me, field, part, land, fh, fl, sems):
+    own = pltpu.make_async_copy(field.at[:, pl.ds(8 * me, 8), :], land.at[0], sems.at[0, 0])
+    own.start()
+    copies = {}
+    for d in A2A_ORDER:
+        peer = me ^ d
+        copies[d] = push(field.at[:, pl.ds(8 * peer, 8), :], land.at[d], sems, d, {"gx": peer})
+
+    def halves(d):
+        rows = pl.ds(pl.multiple_of((me ^ d) * 128, 128), 128)
+        for a in range(8):
+            high, low = split(land[d, :, a, :])
+            fh[rows, 128 * a : 128 * a + 128] = high
+            fl[rows, 128 * a : 128 * a + 128] = low
+
+    own.wait()
+    halves(0)
+    for d in A2A_ORDER:
+        copies[d].wait_recv()
+        halves(d)
+    for panel in range(4):
+        c = 256 * panel
+        bh, bl = fh[c : c + 256, :], fl[c : c + 256, :]
+        ah, al = fh[c:, :], fl[c:, :]
+        block = dg(ah, bh, 1, 1) + dg(ah, bl, 1, 1) + dg(al, bh, 1, 1)
+        for j in (2 * panel, 2 * panel + 1):
+            for i in range(j, 8):
+                top = first_row(i, j)
+                part[top : top + 128, :] = block[128 * i - c : 128 * i - c + 128, 128 * j - c : 128 * j - c + 128]
+    for d in A2A_ORDER:
+        copies[d].wait_send()
+
+
+def reduce_all(place, part, full, land0, land1, land2, land3, sems):
+    core = place.core
+    mine = core * HALF
+    pending = []
+
+    def send(src, dst, k, peer):
+        copy = push(src, dst, sems, k, peer)
+        pending.append(copy)
+        return copy
+
+    def rows(ref, start, size):
+        return ref.at[pl.ds(pl.multiple_of(start, 16), size), :]
+
+    def bases(s):
+        a, b, _ = (place.at[axis] for axis in STREAMS[s])
+        top = mine + THIRD * s
+        return top, top + PIECE * a, top + PIECE * a + BIT * b
+
+    def add(start, size, terms):
+        where = pl.ds(pl.multiple_of(start, 16), size)
+        part[where, :] = part[where, :] + terms
+
+    k = 0
+    swap, first, second, third, back, again, last = [], {}, {}, {}, {}, {}, []
+    for s in range(3):
+        other = (1 - core) * HALF + THIRD * s
+        swap.append(send(rows(part, other, THIRD), rows(land0, THIRD * s, THIRD), k, place.partner()))
+        k += 1
+    for s in range(3):
+        swap[s].wait_recv()
+        top, _, _ = bases(s)
+        add(top, THIRD, land0[THIRD * s : THIRD * s + THIRD, :])
+        axis = STREAMS[s][0]
+        for e in (2, 1, 3):
+            to = (place.at[axis] + e) % 4
+            slot = (3 * s + 3 - e) * PIECE
+            first[s, e] = send(rows(part, top + PIECE * to, PIECE), rows(land1, slot, PIECE), k, place.along(axis, e))
+            k += 1
+    for s in range(3):
+        for e in (2, 1, 3):
+            first[s, e].wait_recv()
+        _, mid, _ = bases(s)
+        got = [land1[(3 * s + t) * PIECE : (3 * s + t + 1) * PIECE, :] for t in range(3)]
+        add(mid, PIECE, got[0] + got[1] + got[2])
+        axis = STREAMS[s][1]
+        for e in (2, 1, 3):
+            to = (place.at[axis] + e) % 4
+            slot = (3 * s + 3 - e) * BIT
+            second[s, e] = send(rows(part, mid + BIT * to, BIT), rows(land2, slot, BIT), k, place.along(axis, e))
+            k += 1
+    for s in range(3):
+        for e in (2, 1, 3):
+            second[s, e].wait_recv()
+        _, _, low = bases(s)
+        got = [land2[(3 * s + t) * BIT : (3 * s + t + 1) * BIT, :] for t in range(3)]
+        add(low, BIT, got[0] + got[1] + got[2])
+        axis = STREAMS[s][2]
+        for e in (2, 1, 3):
+            slot = (3 * s + 3 - e) * BIT
+            third[s, e] = send(rows(part, low, BIT), rows(land3, slot, BIT), k, place.along(axis, e))
+            k += 1
+    for s in range(3):
+        for e in (2, 1, 3):
+            third[s, e].wait_recv()
+        _, _, low = bases(s)
+        got = [land3[(3 * s + t) * BIT : (3 * s + t + 1) * BIT, :] for t in range(3)]
+        even = place.at[STREAMS[s][2]] % 2 == 0
+        where = pl.ds(pl.multiple_of(low, 16), BIT)
+        near = jnp.where(even, got[0], got[2])
+        far = jnp.where(even, got[2], got[0])
+        full[where, :] = (part[where, :] + near) + (got[1] + far)
+        axis = STREAMS[s][1]
+        for e in (2, 1, 3):
+            back[s, e] = send(rows(full, low, BIT), rows(full, low, BIT), k, place.along(axis, e))
+            k += 1
+    for s in range(3):
+        for e in (2, 1, 3):
+            back[s, e].wait_recv()
+        _, mid, _ = bases(s)
+        axis = STREAMS[s][0]
+        for e in (2, 1, 3):
+            again[s, e] = send(rows(full, mid, PIECE), rows(full, mid, PIECE), k, place.along(axis, e))
+            k += 1
+        last.append(send(rows(full, mid, PIECE), rows(full, mid, PIECE), k, place.partner()))
+        k += 1
+    for s in range(3):
+        top, _, _ = bases(s)
+        for e in (1, 3, 2):
+            again[s, e].wait_recv()
+
+            came = (place.at[STREAMS[s][0]] + 4 - e) % 4
+            piece = top + PIECE * came
+            last.append(send(rows(full, piece, PIECE), rows(full, piece, PIECE), k, place.partner()))
+            k += 1
+    for copy in last:
+        copy.wait_recv()
+    for copy in pending:
+        copy.wait_send()
+
+
+N_COPIES = 3 + 9 * 3 + 9 + 12 + 9
+
+
+def gram_kernel(field, full, fh_out, fl_out, land, fh, fl, part, land0, land1, land2, land3, sems, more, keep):
+    place = Place()
+    me = place.gx
+    peers = [{"gx": me ^ d} for d in range(1, 8)] + [place.partner()]
+    peers += [place.along("z", e) for e in (1, 2, 3)] + [place.along("x", e) for e in (1, 3)]
+    greet(peers)
+    gather_products(me, field, part, land, fh, fl, sems)
+    out = [pltpu.make_async_copy(fh, fh_out, keep.at[0]), pltpu.make_async_copy(fl, fl_out, keep.at[1])]
+    for copy in out:
+        copy.start()
+    reduce_all(place, part, full, land0, land1, land2, land3, more)
+    for copy in out:
+        copy.wait()
+
+
+def gram_of(field):
+    rows, order = field.shape[0], 1024
+    hbm, vmem = pl.BlockSpec(memory_space=pl.ANY), pl.BlockSpec(memory_space=pltpu.VMEM)
+    kept = jax.ShapeDtypeStruct((order, order), BF16)
+    return pl.pallas_call(
+        gram_kernel,
+        out_shape=(jax.ShapeDtypeStruct((2 * HALF, 128), F32), kept, kept),
+        in_specs=[hbm],
+        out_specs=(vmem, hbm, hbm),
+        scratch_shapes=[
+            pltpu.VMEM((8, rows, 8, 128), F32),
+            pltpu.VMEM((order, order), BF16),
+            pltpu.VMEM((order, order), BF16),
+            pltpu.VMEM((2 * HALF, 128), F32),
+            pltpu.VMEM((HALF, 128), F32),
+            pltpu.VMEM((9 * PIECE, 128), F32),
+            pltpu.VMEM((9 * BIT, 128), F32),
+            pltpu.VMEM((9 * BIT, 128), F32),
+            pltpu.SemaphoreType.DMA((2, 8)),
+            pltpu.SemaphoreType.DMA((2, N_COPIES)),
+            pltpu.SemaphoreType.DMA((2,)),
+        ],
+        compiler_params=pltpu.CompilerParams(collective_id=0, has_side_effects=True, vmem_limit_bytes=56 << 20),
+    )(field)
+
+
 def iteration_kernel(gram_ref, start_ref, out_ref, gram_high, gram_low, aug, basis):
-    high, low = split(gram_ref[...])
-    gram_high[...] = high
-    gram_low[...] = low
+    for i in range(8):
+        for j in range(i + 1):
+            block = gram_ref[first_row(i, j) : first_row(i, j) + 128, :]
+            places = [(i, j, block)] if i == j else [(i, j, block), (j, i, block.T)]
+            for r, c, value in places:
+                where = (slice(128 * r, 128 * r + 128), slice(128 * c, 128 * c + 128))
+                gram_high[where], gram_low[where] = split(value)
     basis[...] = start_ref[...]
     n = aug.shape[0]
     shape = (n, n)
@@ -95,18 +320,46 @@
     )(gram, start)
 
 
+def core_kernel(basis_ref, fh, fl, core, scaled, cols, sems):
+    me = lax.axis_index("gx")
+    greet([{"gx": me ^ d} for d in range(1, 8)])
+    high, low = split(basis_ref[...])
+    flat = cols.reshape(1024, 128)
+    for a in range(0, 8, 2):
+        c = slice(128 * a, 128 * a + 256)
+        part = dg(high, fh[:, c], 0, 0) + dg(high, fl[:, c], 0, 0) + dg(low, fh[:, c], 0, 0)
+        flat[pl.ds(a, 128, stride=8), :] = part[:, :128]
+        flat[pl.ds(a + 1, 128, stride=8), :] = part[:, 128:]
+    copies = []
+    here = pl.ds(pl.multiple_of(8 * me, 8), 8)
+    for d in A2A_ORDER:
+        peer = me ^ d
+        copies.append(push(cols.at[pl.ds(16 * peer, 16)], core.at[:, here, :], sems, d, {"gx": peer}))
+    own = pltpu.make_async_copy(cols.at[pl.ds(16 * me, 16)], core.at[:, here, :], sems.at[0, 0])
+    own.start()
+    scaled[...] = basis_ref[pl.ds(pl.multiple_of(128 * me, 128), 128), :] * jnp.sqrt(F32(1024))
+    own.wait()
+    for copy in copies:
+        copy.wait()
+
+
+def core_of(basis, fh, fl):
+    vmem = pl.BlockSpec(memory_space=pltpu.VMEM)
+    return pl.pallas_call(
+        core_kernel,
+        out_shape=(jax.ShapeDtypeStruct((16, 64, 128), F32), jax.ShapeDtypeStruct((128, 128), F32)),
+        in_specs=[vmem] * 3,
+        out_specs=(vmem, vmem),
+        scratch_shapes=[pltpu.VMEM((128, 8, 128), F32), pltpu.SemaphoreType.DMA((2, 8))],
+        compiler_params=pltpu.CompilerParams(collective_id=1, has_side_effects=True, vmem_limit_bytes=40 << 20),
+    )(basis, fh, fl)
+
+
 def body(field, start_basis):
-    rows_x, cells_y, cells_z = field.shape
-    flat = field.reshape(rows_x, cells_y * cells_z)
-    fibres = lax.all_to_all(flat, "gx", split_axis=1, concat_axis=0, tiled=True)
-    partial_gram = jnp.dot(fibres, fibres.T, precision=lax.Precision.HIGH, preferred_element_type=F32)
-    gram = lax.psum(partial_gram, ("gx", "gy", "gz"))
+    gram, fh, fl = gram_of(field)
     basis = iterate(gram, start_basis)
-    own_rows = lax.dynamic_slice_in_dim(basis, lax.axis_index("gx") * rows_x, rows_x, 0)
-    scaled_basis = own_rows * jnp.sqrt(jnp.float32(basis.shape[0]))
-    core_cols = jnp.dot(basis.T, fibres, precision=lax.Precision.HIGH, preferred_element_type=F32)
-    core = lax.all_to_all(core_cols, "gx", split_axis=0, concat_axis=1, tiled=True)
-    return (scaled_basis, core.reshape(core.shape[0], cells_y, cells_z))
+    core, scaled_basis = core_of(basis, fh, fl)
+    return (scaled_basis, core)
 
 
 def solution(mesh):

time: 354 us -> 208 us (0.59)
  waiting for transfers between devices: 163 us -> 0 us
  Pallas kernels: 84.5 us -> 203 us
  blocking collectives: 57.3 us -> 0 us
  between operations: 14.1 us -> 0.69 us
  matrix products: 12.6 us -> 0 us
  local copies, waits for them, and re-layouts: 15 us -> 4.68 us
  starting transfers between devices: 4.76 us -> 0 us
    psum x1 -> x0, waiting for transfers between devices: 154 us -> none  [body(): gram = lax.psum(partial_gram, ('gx', 'gy', 'gz'))]
    pallas_call x0 -> x2, Pallas kernels: none -> 118 us  [the longest x1 105 us: gram_of(): pl.pallas_call(gram_kernel, out_shape=(jax.ShapeDtypeStruct((2 * HALF, 12...]
    all_to_all x1 -> x0, blocking collectives: 57.3 us -> none  [body(): fibres = lax.all_to_all(flat, 'gx', split_axis=1, concat_axis=0, tiled=True)]
    dot_general x2 -> x0, matrix products: 12.6 us -> none  [the longest x1 8.31 us: body(): jnp.dot(fibres, fibres.T, precision=lax.Precision.HIGH, preferred_element...]
    all_to_all x3 -> x0, local copies, waits for them, and re-layouts: 9.8 us -> none  [the longest x2 9.49 us: body(): fibres = lax.all_to_all(flat, 'gx', split_axis=1, concat_axis=0, tiled=True)]
    all_to_all x1 -> x0, waiting for transfers between devices: 9.23 us -> none  [body(): lax.all_to_all(core_cols, 'gx', split_axis=0, concat_axis=1, tiled=True)]
    all_to_all x1 -> x0, starting transfers between devices: 4.72 us -> none  [body(): lax.all_to_all(core_cols, 'gx', split_axis=0, concat_axis=1, tiled=True)]
  transfers between devices with their start and end apart: 2 -> 0, of which waited for: 2 -> 0; matrix products, arithmetic and copies ran while one was open for 0% -> 0% of each run, Pallas kernels for 0% -> 0%
where the time goes in v2:
time: 208 us
  Pallas kernels  203 us (98%)
  local copies, waits for them, and re-layouts  4.68 us (2%)
    pallas_call x1, Pallas kernels, gram_of(): pl.pallas_call(gram_kernel, out_shape=(jax.ShapeDtypeStruct((2 * HALF, 12...  105 us
    pallas_call x1, Pallas kernels, iterate(): pl.pallas_call(iteration_kernel, out_shape=jax.ShapeDtypeStruct((order, r...  84.6 us
    pallas_call x1, Pallas kernels, core_of(): pl.pallas_call(core_kernel, out_shape=(jax.ShapeDtypeStruct((16, 64, 128)...  13.2 us
    unnamed x10, local copies, waits for them, and re-layouts  4.68 us

profile of v2, /device:TPU:1, one launch (start us, length us, event | category | flops | bytes accessed | tf_op | source)
XLA Modules:
  0.0 208.1 jit_solution(15454642003319444132)
XLA Ops:
  0.6 0.0 copy-start.3
  0.6 104.9 %shard_map.41 = (f32[4608,128]{1,0:T(8,128)}, bf16[1024,1024]{1,0:T(8,128)(2,1)}, bf16[1024,1024]{1,0:T(8,128)(2,1)}) custom-call(f32[128,64,128]{2,1,0:T(8,128)} %field.1), custom_call_target="tpu_custom_call" | custom-call | tf_op jit(solution)/shard_map/pallas_call | solution.py:252
  105.6 0.0 copy-done.3
  105.6 0.0 copy-start
  105.6 1.7 copy-done
  107.3 0.0 copy-start.1
  107.3 84.6 %shard_map.42.basis_ref = f32[1024,128]{1,0:T(8,128)S(1)} custom-call(f32[4608,128]{1,0:T(8,128)S(1)} %copy-done, f32[1024,128]{1,0:T(8,128)S(1)} %copy-done.3), custom_call_target="tpu_custom_call" | custom-call | tf_op jit(solution)/shard_map/pallas_call | solution.py:308
  191.9 0.0 copy-done.1
  191.9 0.0 copy-start.2
  191.9 1.6 copy-done.2
  193.5 13.2 %shard_map.43 = (f32[16,64,128]{2,1,0:T(8,128)S(1)}, f32[128,128]{1,0:T(8,128)S(1)}) custom-call(f32[1024,128]{1,0:T(8,128)S(1)} %shard_map.42.basis_ref, bf16[1024,1024]{1,0:T(8,128)(2,1)S(1)} %copy-done.1, bf16[1024,1024]{1,0:T(8,128)(2,1)S(1)} %copy-done.2), custom_call_target="tpu_custom_call" | custom-call | tf_op jit(solution)/shard_map/pallas_call | solution.py:348
  206.7 0.6 copy.6
  207.4 0.8 copy.7
Async XLA Ops:
  0.6 105.0 %copy-start.3 = (f32[1024,128]{1,0:T(8,128)S(1)}, f32[1024,128]{1,0:T(8,128)}, u32[]{:S(2)}) copy-start(f32[1024,128]{1,0:T(8,128)} %start_ref.1) | copy-start | bytes 1572868
  105.6 1.7 copy-start
  107.3 84.6 %copy-start.1 = (bf16[1024,1024]{1,0:T(8,128)(2,1)S(1)}, bf16[1024,1024]{1,0:T(8,128)(2,1)}, u32[]{:S(2)}) copy-start(bf16[1024,1024]{1,0:T(8,128)(2,1)} %get-tuple-element.8.fh) | copy-start | bytes 6291460
  191.9 1.6 copy-start.2

commit v3 on v2

--- a/solution.py
+++ b/solution.py
@@ -22,7 +22,14 @@
     return lax.dot_general(a, b, (((ca,), (cb,)), ((), ())), preferred_element_type=F32)
 
 
-def lower_inverse(aug, panel=8):
+def split3(x):
+    high = x.astype(BF16)
+    rest = x - high.astype(F32)
+    mid = rest.astype(BF16)
+    return high, mid, (rest - mid.astype(F32)).astype(BF16)
+
+
+def lower_inverse(aug, panel=16):
     n = aug.shape[0]
     row = lax.broadcasted_iota(jnp.int32, (panel, n), 0)
     for first in range(0, n, panel):
@@ -41,13 +48,10 @@
         left, right = left * scale, right * scale
         aug[first : first + panel, n:] = right
         if first + panel < n:
-            update = lax.dot_general(
-                left,
-                jnp.concatenate([left, right], axis=1),
-                (((0,), (0,)), ((), ())),
-                precision=lax.Precision.HIGHEST,
-                preferred_element_type=F32,
-            )
+            high, mid, low = split3(jnp.concatenate([left, right], axis=1))
+            a = jnp.concatenate([part[:, :n] for part in (high, high, mid, high, low, mid)], axis=0)
+            b = jnp.concatenate([high, mid, high, low, high, mid], axis=0)
+            update = dg(a, b, 0, 0)
             aug[first + panel :, :] = aug[first + panel :, :] - update[first + panel :, :]
 
 

time: 208 us -> 169 us (0.81)
  Pallas kernels: 203 us -> 164 us
    pallas_call x1, Pallas kernels: 84.6 us -> 45.5 us  [iterate(): pl.pallas_call(iteration_kernel, out_shape=jax.ShapeDtypeStruct((order, r...]
where the time goes in v3:
time: 169 us
  Pallas kernels  164 us (97%)
  local copies, waits for them, and re-layouts  4.68 us (3%)
    pallas_call x1, Pallas kernels, gram_of(): pl.pallas_call(gram_kernel, out_shape=(jax.ShapeDtypeStruct((2 * HALF, 12...  105 us
    pallas_call x1, Pallas kernels, iterate(): pl.pallas_call(iteration_kernel, out_shape=jax.ShapeDtypeStruct((order, r...  45.5 us
    pallas_call x1, Pallas kernels, core_of(): pl.pallas_call(core_kernel, out_shape=(jax.ShapeDtypeStruct((16, 64, 128)...  13.2 us
    unnamed x10, local copies, waits for them, and re-layouts  4.68 us

profile of v3, /device:TPU:1, one launch (start us, length us, event | category | flops | bytes accessed | tf_op | source)
XLA Modules:
  0.0 169.0 jit_solution(4100751711949658917)
XLA Ops:
  0.6 0.0 copy-start.3
  0.6 104.9 %shard_map.41 = (f32[4608,128]{1,0:T(8,128)}, bf16[1024,1024]{1,0:T(8,128)(2,1)}, bf16[1024,1024]{1,0:T(8,128)(2,1)}) custom-call(f32[128,64,128]{2,1,0:T(8,128)} %field.1), custom_call_target="tpu_custom_call" | custom-call | tf_op jit(solution)/shard_map/pallas_call | solution.py:256
  105.6 0.0 copy-done.3
  105.6 0.0 copy-start
  105.6 1.7 copy-done
  107.3 0.0 copy-start.1
  107.3 45.5 %shard_map.42.basis_ref = f32[1024,128]{1,0:T(8,128)S(1)} custom-call(f32[4608,128]{1,0:T(8,128)S(1)} %copy-done, f32[1024,128]{1,0:T(8,128)S(1)} %copy-done.3), custom_call_target="tpu_custom_call" | custom-call | tf_op jit(solution)/shard_map/pallas_call | solution.py:312
  152.7 0.0 copy-done.1
  152.7 0.0 copy-start.2
  152.8 1.6 copy-done.2
  154.3 13.2 %shard_map.43 = (f32[16,64,128]{2,1,0:T(8,128)S(1)}, f32[128,128]{1,0:T(8,128)S(1)}) custom-call(f32[1024,128]{1,0:T(8,128)S(1)} %shard_map.42.basis_ref, bf16[1024,1024]{1,0:T(8,128)(2,1)S(1)} %copy-done.1, bf16[1024,1024]{1,0:T(8,128)(2,1)S(1)} %copy-done.2), custom_call_target="tpu_custom_call" | custom-call | tf_op jit(solution)/shard_map/pallas_call | solution.py:352
  167.5 0.6 copy.6
  168.2 0.8 copy.7
Async XLA Ops:
  0.6 105.0 %copy-start.3 = (f32[1024,128]{1,0:T(8,128)S(1)}, f32[1024,128]{1,0:T(8,128)}, u32[]{:S(2)}) copy-start(f32[1024,128]{1,0:T(8,128)} %start_ref.1) | copy-start | bytes 1572868
  105.6 1.7 copy-start
  107.3 45.5 %copy-start.1 = (bf16[1024,1024]{1,0:T(8,128)(2,1)S(1)}, bf16[1024,1024]{1,0:T(8,128)(2,1)}, u32[]{:S(2)}) copy-start(bf16[1024,1024]{1,0:T(8,128)(2,1)} %get-tuple-element.8.fh) | copy-start | bytes 6291460
  152.7 1.6 copy-start.2

commit v4 on v3

--- a/solution.py
+++ b/solution.py
@@ -92,10 +92,15 @@
 STREAMS = (("z", "y", "x"), ("y", "x", "z"), ("x", "z", "y"))
 HALF, THIRD, PIECE, BIT = 2304, 768, 192, 48
 A2A_ORDER = (1, 2, 6, 4, 5, 3, 7)
+ARRIVAL = (0,) + A2A_ORDER
 
 
 def first_row(i, j):
     return (i * (i + 1) // 2 + j) * 128
+
+
+def row_block(k):
+    return pl.ds(pl.multiple_of(k * 128, 128), 128)
 
 
 def gather_products(me, field, part, land, fh, fl, sems):
@@ -105,28 +110,27 @@
     for d in A2A_ORDER:
         peer = me ^ d
         copies[d] = push(field.at[:, pl.ds(8 * peer, 8), :], land.at[d], sems, d, {"gx": peer})
-
-    def halves(d):
-        rows = pl.ds(pl.multiple_of((me ^ d) * 128, 128), 128)
+    for s, d in enumerate(ARRIVAL):
+        if d == 0:
+            own.wait()
+        else:
+            copies[d].wait_recv()
+        here = slice(128 * s, 128 * s + 128)
         for a in range(8):
             high, low = split(land[d, :, a, :])
-            fh[rows, 128 * a : 128 * a + 128] = high
-            fl[rows, 128 * a : 128 * a + 128] = low
-
-    own.wait()
-    halves(0)
-    for d in A2A_ORDER:
-        copies[d].wait_recv()
-        halves(d)
-    for panel in range(4):
-        c = 256 * panel
-        bh, bl = fh[c : c + 256, :], fl[c : c + 256, :]
-        ah, al = fh[c:, :], fl[c:, :]
-        block = dg(ah, bh, 1, 1) + dg(ah, bl, 1, 1) + dg(al, bh, 1, 1)
-        for j in (2 * panel, 2 * panel + 1):
-            for i in range(j, 8):
-                top = first_row(i, j)
-                part[top : top + 128, :] = block[128 * i - c : 128 * i - c + 128, 128 * j - c : 128 * j - c + 128]
+            fh[here, 128 * a : 128 * a + 128] = high
+            fl[here, 128 * a : 128 * a + 128] = low
+        upto = slice(0, 128 * s + 128)
+        both = dg(fh[upto, :], jnp.concatenate([fh[here, :], fl[here, :]], axis=0), 1, 1)
+        block = both[:, :128] + both[:, 128:] + dg(fl[upto, :], fh[here, :], 1, 1)
+        j = me ^ d
+        for t in range(s + 1):
+            i = me ^ ARRIVAL[t]
+            value = block[128 * t : 128 * t + 128, :]
+            if t < s:
+                value = jnp.where(i > j, value, value.T)
+            top = first_row(jnp.maximum(i, j), jnp.minimum(i, j))
+            part[pl.ds(pl.multiple_of(top, 128), 128), :] = value
     for d in A2A_ORDER:
         copies[d].wait_send()
 
@@ -234,48 +238,7 @@
 N_COPIES = 3 + 9 * 3 + 9 + 12 + 9
 
 
-def gram_kernel(field, full, fh_out, fl_out, land, fh, fl, part, land0, land1, land2, land3, sems, more, keep):
-    place = Place()
-    me = place.gx
-    peers = [{"gx": me ^ d} for d in range(1, 8)] + [place.partner()]
-    peers += [place.along("z", e) for e in (1, 2, 3)] + [place.along("x", e) for e in (1, 3)]
-    greet(peers)
-    gather_products(me, field, part, land, fh, fl, sems)
-    out = [pltpu.make_async_copy(fh, fh_out, keep.at[0]), pltpu.make_async_copy(fl, fl_out, keep.at[1])]
-    for copy in out:
-        copy.start()
-    reduce_all(place, part, full, land0, land1, land2, land3, more)
-    for copy in out:
-        copy.wait()
-
-
-def gram_of(field):
-    rows, order = field.shape[0], 1024
-    hbm, vmem = pl.BlockSpec(memory_space=pl.ANY), pl.BlockSpec(memory_space=pltpu.VMEM)
-    kept = jax.ShapeDtypeStruct((order, order), BF16)
-    return pl.pallas_call(
-        gram_kernel,
-        out_shape=(jax.ShapeDtypeStruct((2 * HALF, 128), F32), kept, kept),
-        in_specs=[hbm],
-        out_specs=(vmem, hbm, hbm),
-        scratch_shapes=[
-            pltpu.VMEM((8, rows, 8, 128), F32),
-            pltpu.VMEM((order, order), BF16),
-            pltpu.VMEM((order, order), BF16),
-            pltpu.VMEM((2 * HALF, 128), F32),
-            pltpu.VMEM((HALF, 128), F32),
-            pltpu.VMEM((9 * PIECE, 128), F32),
-            pltpu.VMEM((9 * BIT, 128), F32),
-            pltpu.VMEM((9 * BIT, 128), F32),
-            pltpu.SemaphoreType.DMA((2, 8)),
-            pltpu.SemaphoreType.DMA((2, N_COPIES)),
-            pltpu.SemaphoreType.DMA((2,)),
-        ],
-        compiler_params=pltpu.CompilerParams(collective_id=0, has_side_effects=True, vmem_limit_bytes=56 << 20),
-    )(field)
-
-
-def iteration_kernel(gram_ref, start_ref, out_ref, gram_high, gram_low, aug, basis):
+def iterate(gram_ref, start_ref, gram_high, gram_low, aug, basis):
     for i in range(8):
         for j in range(i + 1):
             block = gram_ref[first_row(i, j) : first_row(i, j) + 128, :]
@@ -304,30 +267,10 @@
         return carry
 
     lax.fori_loop(0, ITERS, step, 0)
-    out_ref[...] = basis[...]
-
-
-def iterate(gram, start):
-    order, rank = start.shape
-    return pl.pallas_call(
-        iteration_kernel,
-        out_shape=jax.ShapeDtypeStruct((order, rank), F32),
-        in_specs=[pl.BlockSpec(memory_space=pltpu.VMEM)] * 2,
-        out_specs=pl.BlockSpec(memory_space=pltpu.VMEM),
-        scratch_shapes=[
-            pltpu.VMEM((order, order), BF16),
-            pltpu.VMEM((order, order), BF16),
-            pltpu.VMEM((rank, 2 * rank), F32),
-            pltpu.VMEM((order, rank), F32),
-        ],
-        compiler_params=pltpu.CompilerParams(vmem_limit_bytes=48 << 20),
-    )(gram, start)
-
-
-def core_kernel(basis_ref, fh, fl, core, scaled, cols, sems):
-    me = lax.axis_index("gx")
-    greet([{"gx": me ^ d} for d in range(1, 8)])
-    high, low = split(basis_ref[...])
+
+
+def project(me, basis, fh, fl, core, cols, sems):
+    high, low = split(jnp.concatenate([basis[row_block(me ^ d), :] for d in ARRIVAL], axis=0))
     flat = cols.reshape(1024, 128)
     for a in range(0, 8, 2):
         c = slice(128 * a, 128 * a + 256)
@@ -341,28 +284,54 @@
         copies.append(push(cols.at[pl.ds(16 * peer, 16)], core.at[:, here, :], sems, d, {"gx": peer}))
     own = pltpu.make_async_copy(cols.at[pl.ds(16 * me, 16)], core.at[:, here, :], sems.at[0, 0])
     own.start()
-    scaled[...] = basis_ref[pl.ds(pl.multiple_of(128 * me, 128), 128), :] * jnp.sqrt(F32(1024))
-    own.wait()
+    return [own] + copies
+
+
+def tucker_kernel(field, start, core, scaled, *scratch):
+    land, fh, fl, part, full, land0, land1, land2, land3, gram_high, gram_low, aug, basis, cols, sems, more, final = scratch
+    place = Place()
+    me = place.gx
+    peers = [{"gx": me ^ d} for d in range(1, 8)] + [place.partner()]
+    peers += [place.along("z", e) for e in (1, 2, 3)] + [place.along("x", e) for e in (1, 3)]
+    greet(peers)
+    gather_products(me, field, part, land, fh, fl, sems)
+    reduce_all(place, part, full, land0, land1, land2, land3, more)
+    iterate(full, start, gram_high, gram_low, aug, basis)
+    copies = project(me, basis, fh, fl, core, cols, final)
+    scaled[...] = basis[row_block(me), :] * jnp.sqrt(F32(1024))
     for copy in copies:
         copy.wait()
 
 
-def core_of(basis, fh, fl):
+def body(field, start_basis):
+    rows, (order, rank) = field.shape[0], start_basis.shape
     vmem = pl.BlockSpec(memory_space=pltpu.VMEM)
-    return pl.pallas_call(
-        core_kernel,
+    core, scaled_basis = pl.pallas_call(
+        tucker_kernel,
         out_shape=(jax.ShapeDtypeStruct((16, 64, 128), F32), jax.ShapeDtypeStruct((128, 128), F32)),
-        in_specs=[vmem] * 3,
+        in_specs=[pl.BlockSpec(memory_space=pl.ANY), vmem],
         out_specs=(vmem, vmem),
-        scratch_shapes=[pltpu.VMEM((128, 8, 128), F32), pltpu.SemaphoreType.DMA((2, 8))],
-        compiler_params=pltpu.CompilerParams(collective_id=1, has_side_effects=True, vmem_limit_bytes=40 << 20),
-    )(basis, fh, fl)
-
-
-def body(field, start_basis):
-    gram, fh, fl = gram_of(field)
-    basis = iterate(gram, start_basis)
-    core, scaled_basis = core_of(basis, fh, fl)
+        scratch_shapes=[
+            pltpu.VMEM((8, rows, 8, 128), F32),
+            pltpu.VMEM((order, order), BF16),
+            pltpu.VMEM((order, order), BF16),
+            pltpu.VMEM((2 * HALF, 128), F32),
+            pltpu.VMEM((2 * HALF, 128), F32),
+            pltpu.VMEM((HALF, 128), F32),
+            pltpu.VMEM((9 * PIECE, 128), F32),
+            pltpu.VMEM((9 * BIT, 128), F32),
+            pltpu.VMEM((9 * BIT, 128), F32),
+            pltpu.VMEM((order, order), BF16),
+            pltpu.VMEM((order, order), BF16),
+            pltpu.VMEM((rank, 2 * rank), F32),
+            pltpu.VMEM((order, rank), F32),
+            pltpu.VMEM((128, 8, 128), F32),
+            pltpu.SemaphoreType.DMA((2, 8)),
+            pltpu.SemaphoreType.DMA((2, N_COPIES)),
+            pltpu.SemaphoreType.DMA((2, 8)),
+        ],
+        compiler_params=pltpu.CompilerParams(collective_id=0, has_side_effects=True, vmem_limit_bytes=56 << 20),
+    )(field, start_basis)
     return (scaled_basis, core)
 
 

time: 169 us -> 164 us (0.970)
  Pallas kernels: 164 us -> 160 us
    pallas_call x3 -> x1, Pallas kernels: 164 us -> 160 us  [body(): pl.pallas_call(tucker_kernel, out_shape=(jax.ShapeDtypeStruct((16, 64, 12...]
    unnamed x10 -> x2, local copies, waits for them, and re-layouts: 4.68 us -> 3.36 us
where the time goes in v4:
time: 164 us
  Pallas kernels  160 us (98%)
  local copies, waits for them, and re-layouts  3.36 us (2%)
    pallas_call x1, Pallas kernels, body(): pl.pallas_call(tucker_kernel, out_shape=(jax.ShapeDtypeStruct((16, 64, 12...  160 us
    unnamed x2, local copies, waits for them, and re-layouts  3.36 us

profile of v4, /device:TPU:1, one launch (start us, length us, event | category | flops | bytes accessed | tf_op | source)
XLA Modules:
  0.0 163.9 jit_solution(15675715396818483333)
XLA Ops:
  0.6 159.9 %shard_map.41 = (f32[16,64,128]{2,1,0:T(8,128)}, f32[128,128]{1,0:T(8,128)}) custom-call(f32[128,64,128]{2,1,0:T(8,128)} %field.1, f32[1024,128]{1,0:T(8,128)} %start.1), custom_call_target="tpu_custom_call" | custom-call | tf_op jit(solution)/shard_map/pallas_call | solution.py:309
  160.5 1.5 copy.6
  162.0 1.9 %copy.7 = f32[16,64,128]{2,1,0:T(8,128)} copy(f32[16,64,128]{2,1,0:T(8,128)} %get-tuple-element.9) | data formatting | bytes 1048576
